TPU v7x, 32 devices: a whole 2x2x4 slice. The times are simulated.
32 devices in a mesh: row: 4 (over z), col: 4 (over y, core), ch: 2 (over x).
Axes of the slice: x: 2, y: 2, z: 4, core: 2. Of those that a mesh axis runs over, the one named last changes fastest.
Arguments:
- spectra: float32 [384, 128, 1024], P('ch', 'row', 'col'), may hold values from 0 to 1
- pixel_factor: float32 [64, 128, 1024], P(None, 'row', 'col'), may hold values from 0.1 to 1
- channel_factor: float32 [64, 384], P(None, 'ch'), may hold values from 0.1 to 1
- labels: int32 [128, 1024], P('row', 'col'), may hold values from 0 to 3
Outputs:
- smoothed_factor: float32 [64, 128, 1024], P(None, 'row', 'col')
- new_channel: float32 [64, 384], P(None, 'ch')
All inputs are finite; a program needn't handle non-finite values.
Results may differ from a plain program's by a relative error of at most 0.000068.
Values sent between devices are 32-bit elements; how exact they have to be, the bound alone decides.
A program may use at most 64 MiB of HBM per device.

v0:
```python
import jax
import jax.numpy as jnp
from jax import lax
from jax.sharding import PartitionSpec as P

SMOOTH = 3
epsilon = 1e-09


def padded_2(block, sides, width):
    for axis, dim in sides:
        count = lax.axis_size(axis)
        forward = [(i, i + 1) for i in range(count - 1)]
        backward = [(target, source) for source, target in forward]
        low = lax.ppermute(
            lax.slice_in_dim(block, block.shape[dim] - width, None, axis=dim), axis, forward
        )
        high = lax.ppermute(lax.slice_in_dim(block, 0, width, axis=dim), axis, backward)
        block = jnp.concatenate([low, block, high], axis=dim)
    return block


def coefficients(marked):
    center = marked[1:-1, 1:-1]
    result = []
    for neighbour in (marked[:-2, 1:-1], marked[2:, 1:-1], marked[1:-1, :-2], marked[1:-1, 2:]):
        result.append(
            jnp.where(neighbour == 0, 0.0, jnp.where(neighbour == center, 1.0, 0.25)).astype(
                jnp.float32
            )
        )
    return result


def smooth_once(padded, field, weights):
    combined = field + weights[0] * padded[:, :-2, 1:-1] + weights[1] * padded[:, 2:, 1:-1]
    combined = combined + weights[2] * padded[:, 1:-1, :-2] + weights[3] * padded[:, 1:-1, 2:]
    return combined / (1.0 + weights[0] + weights[1] + weights[2] + weights[3])


def lift_factor(own_factor, pixel_top, chan_gram):
    factor_rank = own_factor.shape[0]
    flat_own = own_factor.reshape(factor_rank, -1)
    lower = jnp.dot(
        chan_gram, flat_own, precision=lax.Precision.HIGHEST, preferred_element_type=jnp.float32
    )
    return (flat_own * pixel_top.reshape(factor_rank, -1) / (lower + epsilon)).reshape(
        own_factor.shape
    )


def shards(spectra, pixel_factor, channel_factor, labels):
    precise = lax.Precision.HIGHEST
    contraction = (((1,), (1,)), ((), ()))
    factor_rank, row_count, col_count = pixel_factor.shape
    flat_pixel = pixel_factor.reshape(factor_rank, row_count * col_count)
    flat_data = spectra.reshape(spectra.shape[0], row_count * col_count)
    chan_top = lax.dot_general(
        flat_pixel, flat_data, contraction, precision=precise, preferred_element_type=jnp.float32
    )
    pixel_gram = lax.dot_general(
        flat_pixel, flat_pixel, contraction, precision=precise, preferred_element_type=jnp.float32
    )
    chan_top, pixel_gram = lax.psum((chan_top, pixel_gram), ("row", "col"))
    new_channel = (
        channel_factor
        * chan_top
        / (
            jnp.dot(
                pixel_gram, channel_factor, precision=precise, preferred_element_type=jnp.float32
            )
            + epsilon
        )
    )
    part_top = jnp.dot(
        new_channel, flat_data, precision=precise, preferred_element_type=jnp.float32
    ).reshape(factor_rank, row_count, col_count)
    part_gram = lax.dot_general(
        new_channel, new_channel, contraction, precision=precise, preferred_element_type=jnp.float32
    )
    marked = labels + 1
    share_rows = row_count // lax.axis_size("ch")
    share_start = lax.axis_index("ch") * share_rows
    pixel_top = lax.psum_scatter(part_top, "ch", scatter_dimension=1, tiled=True)
    chan_gram = lax.psum(part_gram, "ch")
    own_factor = lax.dynamic_slice_in_dim(pixel_factor, share_start, share_rows, 1)
    own_marks = lax.dynamic_slice_in_dim(marked, share_start, share_rows, 0)
    field = lift_factor(own_factor, pixel_top, chan_gram)
    border_marks = padded_2(own_marks, ((("row", "ch"), 0), ("col", 1)), 1)
    weights = coefficients(border_marks)
    for iteration in range(SMOOTH):
        padded = padded_2(field, ((("row", "ch"), 1), ("col", 2)), 1)
        field = smooth_once(padded, field, weights)
    smoothed_factor = lax.all_gather(field, "ch", axis=1, tiled=True)
    return (smoothed_factor, new_channel)


def solution(mesh):
    placed = (P("ch", "row", "col"), P(None, "row", "col"), P(None, "ch"), P("row", "col"))
    return jax.shard_map(
        shards,
        mesh=mesh,
        in_specs=placed,
        out_specs=(P(None, "row", "col"), P(None, "ch")),
        check_vma=False,
    )
```

profile of v0, /device:TPU:0, one launch (start us, length us, event | category | flops | bytes accessed | tf_op | source)
XLA Modules:
  0.0 290.6 jit_solution(9528814193666715446)
XLA Ops:
  7.2 7.0 %fusion.42 = f32[64,64]{1,0:T(8,128)} fusion(f32[64,32,256]{2,1,0:T(8,128)} %param.5), kind=kOutput, calls=%fused_computation.64 | convolution fusion | flops 402653184 | bytes 2113536 | tf_op jit(solution)/shard_map/dot_general | solution.py:61
  14.2 12.2 %fusion.36 = f32[64,192]{1,0:T(8,128)} fusion(f32[192,32,256]{2,1,0:T(8,128)} %param.4, f32[64,32,256]{2,1,0:T(8,128)S(1)} %copy-done.2), kind=kOutput, calls=%fused_computation.61 | convolution fusion | flops 1207959552 | bytes 8437760 | tf_op jit(solution)/shard_map/dot_general | solution.py:58
  26.7 91.5 %all-reduce.3.cloned.1.call-done = (f32[64,64]{1,0:T(8,128)}, f32[64,192]{1,0:T(8,128)}) async-done(((f32[64,64]{1,0:T(8,128)}, f32[64,192]{1,0:T(8,128)}), (f32[64,64]{1,0:T(8,128)}, f32[64,192]{1,0:T(8,128)})) %all-reduce.3.cloned.1.call-update) | async-done | bytes 65552 | tf_op jit(solution)/shard_map/psum | solution.py:64
  119.3 11.4 %fusion = f32[64,32,256]{2,0,1:T(8,128)} fusion(f32[64,192]{1,0:T(8,128)S(1)} %fusion.41, f32[24,8,32,256]{3,2,1,0:T(8,128)} %bitcast.30), kind=kOutput, calls=%fused_computation | convolution fusion | flops 1207959552 | bytes 8437760 | tf_op jit(solution)/shard_map/dot_general | solution.py:75
  132.8 4.5 %collective-permute-start = (s32[1,256]{1,0:T(1,128)S(1)}, s32[1,256]{1,0:T(1,128)S(1)}, u32[]{:S(2)}, u32[]{:S(2)}) collective-permute-start(s32[1,256]{1,0:T(1,128)S(1)} %get-tuple-element.34), channel_id=1, source_target_pairs={{0,1},{1,8},{8,9},{9,16},{16,17},{17,24},{24,25},{2,3},{3,10},{10,... | collective-permute-start | bytes 3080 | tf_op jit(solution)/shard_map/ppermute | solution.py:15
  138.8 10.2 %psum.23 = f32[64,64]{1,0:T(8,128)S(1)} all-reduce(f32[64,64]{1,0:T(8,128)S(1)} %fusion.55), channel_id=1, replica_groups=mesh['row'=4,'col'=4,'ch'=2] {'ch'}, use_global_device_ids=true, to_apply=%region_3.0 | all-reduce | flops 4096 | bytes 32768 | tf_op jit(solution)/shard_map/psum | solution.py:85
  149.0 13.5 %reduce-scatter.2.cloned.1.call-done = f32[64,16,256]{2,0,1:T(8,128)} async-done(((f32[64,32,256]{2,0,1:T(8,128)}), f32[64,16,256]{2,0,1:T(8,128)}) %reduce-scatter.2.cloned.1.call-update) | async-done | bytes 1048592 | tf_op jit(solution)/shard_map/reduce_scatter | solution.py:84
  166.7 4.5 %collective-permute-start.1 = (f32[64,1,256]{2,0,1:T(8,128)S(1)}, f32[64,1,256]{2,0,1:T(8,128)S(1)}, u32[]{:S(2)}, u32[]{:S(2)}) collective-permute-start(f32[64,1,256]{2,0,1:T(8,128)S(1)} %copy.160), channel_id=1, source_target_pairs={{0,1},{1,8},{8,9},{9,16},{16,17},{17,24},{24,25},{2,3},{3,10},{10,... | collective-permute-start | bytes 196616 | tf_op jit(solution)/shard_map/ppermute | solution.py:15
  172.7 3.0 %collective-permute-start.4 = (s32[18,1]{1,0:T(8,128)S(1)}, s32[18,1]{1,0:T(8,128)S(1)}, u32[]{:S(2)}, u32[]{:S(2)}) collective-permute-start(s32[18,1]{1,0:T(8,128)S(1)} %get-tuple-element.32), channel_id=1, source_target_pairs={{0,2},{2,4},{4,6},{1,3},{3,5},{5,7},{8,10},{10,12},{12,14},{9,11},... | collective-permute-start | bytes 224 | tf_op jit(solution)/shard_map/ppermute | solution.py:15
  175.7 1.6 copy.135
  177.5 3.0 %collective-permute-start.5 = (f32[64,18,1]{0,1,2:T(8,128)S(1)}, f32[64,18,1]{0,1,2:T(8,128)S(1)}, u32[]{:S(2)}, u32[]{:S(2)}) collective-permute-start(f32[64,18,1]{0,1,2:T(8,128)S(1)} %get-tuple-element.23), channel_id=1, source_target_pairs={{0,2},{2,4},{4,6},{1,3},{3,5},{5,7},{8,10},{10,12},{12,14},{9,11},... | collective-permute-start | bytes 13832 | tf_op jit(solution)/shard_map/ppermute | solution.py:15
  183.6 9.2 %fusion.26 = f32[64,16,256]{0,1,2:T(8,128)S(1)} fusion(f32[64,18,1]{0,1,2:T(8,128)S(1)} %collective-permute-done.7, f32[64,1,256]{0,1,2:T(1,128)S(1)} %copy.139, f32[64,16,256]{0,1,2:T(8,128)} %copy-done.1, f32[64,1,256]{0,1,2:T(1,128)S(1)} %copy.133, f32[64,18,1]{0,1,2:T(8,128)S(1)} %collective-permute-done.5, f32[16,256]{0,1:T(8,128)S(1)} %copy.145, ...), kind=kLoop, calls=%fused_computation.44 | loop fusion | flops 4456448 | bytes 2319360 | tf_op jit(solution)/shard_map/div | solution.py:38
  194.5 4.5 %collective-permute-start.8 = (f32[64,1,256]{2,0,1:T(8,128)S(1)}, f32[64,1,256]{2,0,1:T(8,128)S(1)}, u32[]{:S(2)}, u32[]{:S(2)}) collective-permute-start(f32[64,1,256]{2,0,1:T(8,128)S(1)} %copy.146), channel_id=1, source_target_pairs={{0,1},{1,8},{8,9},{9,16},{16,17},{17,24},{24,25},{2,3},{3,10},{10,... | collective-permute-start | bytes 196616 | tf_op jit(solution)/shard_map/ppermute | solution.py:15
  199.4 2.0 collective-permute-done.8
  201.4 2.8 collective-permute-start.10
  205.6 2.4 collective-permute-done.11
  208.0 9.2 %fusion.17 = f32[64,16,256]{0,1,2:T(8,128)S(1)} fusion(f32[64,18,1]{0,1,2:T(8,128)S(1)} %collective-permute-done.11, f32[64,1,256]{0,1,2:T(1,128)S(1)} %copy.149, f32[64,16,256]{0,1,2:T(8,128)} %copy-done, f32[64,1,256]{0,1,2:T(1,128)S(1)} %copy.147, f32[64,18,1]{0,1,2:T(8,128)S(1)} %collective-permute-done.10, f32[16,256]{0,1:T(8,128)S(1)} %copy.145, ...), kind=kLoop, calls=%fused_computation.27 | loop fusion | flops 4456448 | bytes 2319360 | tf_op jit(solution)/shard_map/div | solution.py:38
  218.9 4.9 %collective-permute-start.12 = (f32[64,1,256]{2,0,1:T(8,128)S(1)}, f32[64,1,256]{2,0,1:T(8,128)S(1)}, u32[]{:S(2)}, u32[]{:S(2)}) collective-permute-start(f32[64,1,256]{2,0,1:T(8,128)S(1)} %copy.152), channel_id=1, source_target_pairs={{0,1},{1,8},{8,9},{9,16},{16,17},{17,24},{24,25},{2,3},{3,10},{10,... | collective-permute-start | bytes 196616 | tf_op jit(solution)/shard_map/ppermute | solution.py:15
  225.8 3.6 %collective-permute-start.14 = (f32[64,18,1]{0,1,2:T(8,128)S(1)}, f32[64,18,1]{0,1,2:T(8,128)S(1)}, u32[]{:S(2)}, u32[]{:S(2)}) collective-permute-start(f32[64,18,1]{0,1,2:T(8,128)S(1)} %get-tuple-element.19), channel_id=1, source_target_pairs={{0,2},{2,4},{4,6},{1,3},{3,5},{5,7},{8,10},{10,12},{12,14},{9,11},... | collective-permute-start | bytes 13832 | tf_op jit(solution)/shard_map/ppermute | solution.py:15
  230.7 2.1 collective-permute-done.15
  232.7 5.2 %fusion.8 = f32[64,16,256]{0,1,2:T(8,128)} fusion(f32[64,18,1]{0,1,2:T(8,128)S(1)} %collective-permute-done.15, f32[64,1,256]{0,1,2:T(1,128)S(1)} %copy.155, f32[64,16,256]{0,1,2:T(8,128)S(1)} %fusion.17, f32[64,1,256]{0,1,2:T(1,128)S(1)} %copy.153, f32[64,18,1]{0,1,2:T(8,128)S(1)} %collective-permute-done.14, f32[16,256]{0,1:T(8,128)S(1)} %copy.145, ...), kind=kLoop, calls=%fused_computation.10 | loop fusion | flops 4456448 | bytes 2319360 | tf_op jit(solution)/shard_map/div | solution.py:38
  237.9 3.5 %copy.158 = f32[64,16,256]{2,0,1:T(8,128)} copy(f32[64,16,256]{0,1,2:T(8,128)} %fusion.8) | data formatting | bytes 2097152 | tf_op jit(solution)/shard_map/div | solution.py:38
  241.4 38.5 %all-gather.2.cloned.1.call-done = f32[64,32,256]{2,0,1:T(8,128)} async-done(((f32[64,16,256]{2,0,1:T(8,128)}), f32[64,32,256]{2,0,1:T(8,128)}) %all-gather.2.cloned.1.call-update) | async-done | bytes 2097168 | tf_op jit(solution)/shard_map/all_gather | solution.py:94
  280.0 4.1 %copy.159 = f32[64,32,256]{2,1,0:T(8,128)} copy(f32[64,32,256]{2,0,1:T(8,128)} %all-gather.2.cloned.1.call-done) | data formatting | bytes 4194304
  (74 shorter events, 21.9 us)
Async XLA Ops:
  7.2 7.1 %copy-start.2 = (f32[64,32,256]{2,1,0:T(8,128)S(1)}, f32[64,32,256]{2,1,0:T(8,128)}, u32[]{:S(2)}) copy-start(f32[64,32,256]{2,1,0:T(8,128)} %param.5) | copy-start | bytes 6291460
  7.2 111.1 %all-reduce.3.cloned.1.call-start = ((), (), s32[]{:S(2)}) async-start(), calls=%async_computation.3 | async-start | bytes 196608 | tf_op jit(solution)/shard_map/psum | solution.py:64
  14.2 104.0 %copy-start.5 = (f32[64,192]{1,0:T(8,128)S(1)}, f32[64,192]{1,0:T(8,128)}, u32[]{:S(2)}) copy-start(f32[64,192]{1,0:T(8,128)} %param.6) | copy-start | bytes 147460
  26.5 136.1 %reduce-scatter.2.cloned.1.call-start = ((), (), s32[]{:S(2)}) async-start(), calls=%async_computation.1 | async-start | bytes 3145728 | tf_op jit(solution)/shard_map/reduce_scatter | solution.py:84
  119.3 19.3 %copy-start.3 = (f32[64,192]{1,0:T(8,128)}, f32[64,192]{1,0:T(8,128)S(1)}, u32[]{:S(2)}) copy-start(f32[64,192]{1,0:T(8,128)S(1)} %fusion.41) | copy-start | bytes 147460
  130.7 149.3 %all-gather.2.cloned.1.call-start = ((), (), s32[]{:S(2)}) async-start(), calls=%async_computation.2 | async-start | bytes 3145728 | tf_op jit(solution)/shard_map/all_gather | solution.py:94
  131.5 6.6 %collective-permute-start.2 = (s32[1,256]{1,0:T(1,128)S(1)}, s32[1,256]{1,0:T(1,128)S(1)}, u32[]{:S(2)}, u32[]{:S(2)}) collective-permute-start(s32[1,256]{1,0:T(1,128)S(1)} %get-tuple-element.33), channel_id=1, source_target_pairs={{1,0},{8,1},{9,8},{16,9},{17,16},{24,17},{25,24},{3,2},{10,3},{11,... | collective-permute-start | bytes 3080 | tf_op jit(solution)/shard_map/ppermute | solution.py:18
  132.8 5.8 %collective-permute-start = (s32[1,256]{1,0:T(1,128)S(1)}, s32[1,256]{1,0:T(1,128)S(1)}, u32[]{:S(2)}, u32[]{:S(2)}) collective-permute-start(s32[1,256]{1,0:T(1,128)S(1)} %get-tuple-element.34), channel_id=1, source_target_pairs={{0,1},{1,8},{8,9},{9,16},{16,17},{17,24},{24,25},{2,3},{3,10},{10,... | collective-permute-start | bytes 3080 | tf_op jit(solution)/shard_map/ppermute | solution.py:15
  165.4 11.9 %collective-permute-start.3 = (f32[64,1,256]{2,0,1:T(8,128)S(1)}, f32[64,1,256]{2,0,1:T(8,128)S(1)}, u32[]{:S(2)}, u32[]{:S(2)}) collective-permute-start(f32[64,1,256]{2,0,1:T(8,128)S(1)} %copy.161), channel_id=1, source_target_pairs={{1,0},{8,1},{9,8},{16,9},{17,16},{24,17},{25,24},{3,2},{10,3},{11,... | collective-permute-start | bytes 196616 | tf_op jit(solution)/shard_map/ppermute | solution.py:18
  166.7 10.7 %collective-permute-start.1 = (f32[64,1,256]{2,0,1:T(8,128)S(1)}, f32[64,1,256]{2,0,1:T(8,128)S(1)}, u32[]{:S(2)}, u32[]{:S(2)}) collective-permute-start(f32[64,1,256]{2,0,1:T(8,128)S(1)} %copy.160), channel_id=1, source_target_pairs={{0,1},{1,8},{8,9},{9,16},{16,17},{17,24},{24,25},{2,3},{3,10},{10,... | collective-permute-start | bytes 196616 | tf_op jit(solution)/shard_map/ppermute | solution.py:15
  171.4 10.7 %collective-permute-start.6 = (s32[18,1]{1,0:T(8,128)S(1)}, s32[18,1]{1,0:T(8,128)S(1)}, u32[]{:S(2)}, u32[]{:S(2)}) collective-permute-start(s32[18,1]{1,0:T(8,128)S(1)} %get-tuple-element.31), channel_id=1, source_target_pairs={{2,0},{4,2},{6,4},{3,1},{5,3},{7,5},{10,8},{12,10},{14,12},{11,9},... | collective-permute-start | bytes 224 | tf_op jit(solution)/shard_map/ppermute | solution.py:18
  172.7 9.4 %collective-permute-start.4 = (s32[18,1]{1,0:T(8,128)S(1)}, s32[18,1]{1,0:T(8,128)S(1)}, u32[]{:S(2)}, u32[]{:S(2)}) collective-permute-start(s32[18,1]{1,0:T(8,128)S(1)} %get-tuple-element.32), channel_id=1, source_target_pairs={{0,2},{2,4},{4,6},{1,3},{3,5},{5,7},{8,10},{10,12},{12,14},{9,11},... | collective-permute-start | bytes 224 | tf_op jit(solution)/shard_map/ppermute | solution.py:15
  177.3 5.4 %copy-start.1 = (f32[64,16,256]{0,1,2:T(8,128)}, f32[64,16,256]{0,1,2:T(8,128)S(1)}, u32[]{:S(2)}) copy-start(f32[64,16,256]{0,1,2:T(8,128)S(1)} %copy.135) | copy-start | bytes 3145732
  177.5 5.1 %collective-permute-start.5 = (f32[64,18,1]{0,1,2:T(8,128)S(1)}, f32[64,18,1]{0,1,2:T(8,128)S(1)}, u32[]{:S(2)}, u32[]{:S(2)}) collective-permute-start(f32[64,18,1]{0,1,2:T(8,128)S(1)} %get-tuple-element.23), channel_id=1, source_target_pairs={{0,2},{2,4},{4,6},{1,3},{3,5},{5,7},{8,10},{10,12},{12,14},{9,11},... | collective-permute-start | bytes 13832 | tf_op jit(solution)/shard_map/ppermute | solution.py:15
  180.5 3.1 %collective-permute-start.7 = (f32[64,18,1]{0,1,2:T(8,128)S(1)}, f32[64,18,1]{0,1,2:T(8,128)S(1)}, u32[]{:S(2)}, u32[]{:S(2)}) collective-permute-start(f32[64,18,1]{0,1,2:T(8,128)S(1)} %get-tuple-element.24), channel_id=1, source_target_pairs={{2,0},{4,2},{6,4},{3,1},{5,3},{7,5},{10,8},{12,10},{14,12},{11,9},... | collective-permute-start | bytes 13832 | tf_op jit(solution)/shard_map/ppermute | solution.py:18
  192.8 12.8 %copy-start = (f32[64,16,256]{0,1,2:T(8,128)}, f32[64,16,256]{0,1,2:T(8,128)S(1)}, u32[]{:S(2)}) copy-start(f32[64,16,256]{0,1,2:T(8,128)S(1)} %fusion.26) | copy-start | bytes 3145732
  193.1 6.2 %collective-permute-start.9 = (f32[64,1,256]{2,0,1:T(8,128)S(1)}, f32[64,1,256]{2,0,1:T(8,128)S(1)}, u32[]{:S(2)}, u32[]{:S(2)}) collective-permute-start(f32[64,1,256]{2,0,1:T(8,128)S(1)} %copy.148), channel_id=1, source_target_pairs={{1,0},{8,1},{9,8},{16,9},{17,16},{24,17},{25,24},{3,2},{10,3},{11,... | collective-permute-start | bytes 196616 | tf_op jit(solution)/shard_map/ppermute | solution.py:18
  194.5 6.8 %collective-permute-start.8 = (f32[64,1,256]{2,0,1:T(8,128)S(1)}, f32[64,1,256]{2,0,1:T(8,128)S(1)}, u32[]{:S(2)}, u32[]{:S(2)}) collective-permute-start(f32[64,1,256]{2,0,1:T(8,128)S(1)} %copy.146), channel_id=1, source_target_pairs={{0,1},{1,8},{8,9},{9,16},{16,17},{17,24},{24,25},{2,3},{3,10},{10,... | collective-permute-start | bytes 196616 | tf_op jit(solution)/shard_map/ppermute | solution.py:15
  201.4 4.1 %collective-permute-start.10 = (f32[64,18,1]{0,1,2:T(8,128)S(1)}, f32[64,18,1]{0,1,2:T(8,128)S(1)}, u32[]{:S(2)}, u32[]{:S(2)}) collective-permute-start(f32[64,18,1]{0,1,2:T(8,128)S(1)} %get-tuple-element.21), channel_id=1, source_target_pairs={{0,2},{2,4},{4,6},{1,3},{3,5},{5,7},{8,10},{10,12},{12,14},{9,11},... | collective-permute-start | bytes 13832 | tf_op jit(solution)/shard_map/ppermute | solution.py:15
  204.3 3.7 %collective-permute-start.11 = (f32[64,18,1]{0,1,2:T(8,128)S(1)}, f32[64,18,1]{0,1,2:T(8,128)S(1)}, u32[]{:S(2)}, u32[]{:S(2)}) collective-permute-start(f32[64,18,1]{0,1,2:T(8,128)S(1)} %get-tuple-element.22), channel_id=1, source_target_pairs={{2,0},{4,2},{6,4},{3,1},{5,3},{7,5},{10,8},{12,10},{14,12},{11,9},... | collective-permute-start | bytes 13832 | tf_op jit(solution)/shard_map/ppermute | solution.py:18
  217.5 6.5 %collective-permute-start.13 = (f32[64,1,256]{2,0,1:T(8,128)S(1)}, f32[64,1,256]{2,0,1:T(8,128)S(1)}, u32[]{:S(2)}, u32[]{:S(2)}) collective-permute-start(f32[64,1,256]{2,0,1:T(8,128)S(1)} %copy.154), channel_id=1, source_target_pairs={{1,0},{8,1},{9,8},{16,9},{17,16},{24,17},{25,24},{3,2},{10,3},{11,... | collective-permute-start | bytes 196616 | tf_op jit(solution)/shard_map/ppermute | solution.py:18
  218.9 6.8 %collective-permute-start.12 = (f32[64,1,256]{2,0,1:T(8,128)S(1)}, f32[64,1,256]{2,0,1:T(8,128)S(1)}, u32[]{:S(2)}, u32[]{:S(2)}) collective-permute-start(f32[64,1,256]{2,0,1:T(8,128)S(1)} %copy.152), channel_id=1, source_target_pairs={{0,1},{1,8},{8,9},{9,16},{16,17},{17,24},{24,25},{2,3},{3,10},{10,... | collective-permute-start | bytes 196616 | tf_op jit(solution)/shard_map/ppermute | solution.py:15
  225.8 4.9 %collective-permute-start.14 = (f32[64,18,1]{0,1,2:T(8,128)S(1)}, f32[64,18,1]{0,1,2:T(8,128)S(1)}, u32[]{:S(2)}, u32[]{:S(2)}) collective-permute-start(f32[64,18,1]{0,1,2:T(8,128)S(1)} %get-tuple-element.19), channel_id=1, source_target_pairs={{0,2},{2,4},{4,6},{1,3},{3,5},{5,7},{8,10},{10,12},{12,14},{9,11},... | collective-permute-start | bytes 13832 | tf_op jit(solution)/shard_map/ppermute | solution.py:15
  229.4 3.4 %collective-permute-start.15 = (f32[64,18,1]{0,1,2:T(8,128)S(1)}, f32[64,18,1]{0,1,2:T(8,128)S(1)}, u32[]{:S(2)}, u32[]{:S(2)}) collective-permute-start(f32[64,18,1]{0,1,2:T(8,128)S(1)} %get-tuple-element.20), channel_id=1, source_target_pairs={{2,0},{4,2},{6,4},{3,1},{5,3},{7,5},{10,8},{12,10},{14,12},{11,9},... | collective-permute-start | bytes 13832 | tf_op jit(solution)/shard_map/ppermute | solution.py:18
  (1 other events, 0.8 us)
Sparse Core Ops, SparseCore 0:
  26.6 91.6 all-reduce.2
  130.8 31.6 reduce-scatter.1
  241.6 38.3 all-gather.1
where the time goes:
time: 292 us; the launch traced here: 291 us
  waiting for transfers between devices  154 us (53%)
  starting transfers between devices  41.8 us (14%)
  matrix products  33 us (11%)
  other arithmetic  23.7 us (8%)
  between operations  14.2 us (5%)
  local copies, waits for them, and re-layouts  14.1 us (5%)
  blocking collectives  10.2 us (3%)
    psum x1, waiting for transfers between devices, shards(): chan_top, pixel_gram = lax.psum((chan_top, pixel_gram), ('row', 'col'))  91.5 us
    all_gather x1, waiting for transfers between devices, shards(): smoothed_factor = lax.all_gather(field, 'ch', axis=1, tiled=True)  38.5 us
    ppermute x8, starting transfers between devices, padded_2(): lax.ppermute(lax.slice_in_dim(block, block.shape[dim] - width, None, axis...  31 us
    div x3, other arithmetic, smooth_once(): return combined / (1.0 + weights[0] + weights[1] + weights[2] + weights[3])  23.6 us
    reduce_scatter x1, waiting for transfers between devices, shards(): lax.psum_scatter(part_top, 'ch', scatter_dimension=1, tiled=True)  13.5 us
    dot_general x1, matrix products, shards(): lax.dot_general(flat_pixel, flat_data, contraction, precision=precise, pr...  12.2 us
    dot_general x1, matrix products, shards(): jnp.dot(new_channel, flat_data, precision=precise, preferred_element_type...  11.4 us
    ppermute x8, starting transfers between devices, padded_2(): lax.ppermute(lax.slice_in_dim(block, 0, width, axis=dim), axis, backward)  10.5 us
  transfers between devices with their start and end apart: 19, of which 11 were waited for; matrix products, arithmetic and copies ran while one was open for 1% of the time, Pallas kernels for 0%

commit v1 on v0

--- a/solution.py
+++ b/solution.py
@@ -91,7 +91,9 @@
     for iteration in range(SMOOTH):
         padded = padded_2(field, ((("row", "ch"), 1), ("col", 2)), 1)
         field = smooth_once(padded, field, weights)
-    smoothed_factor = lax.all_gather(field, "ch", axis=1, tiled=True)
+    smoothed_factor = jnp.concatenate(
+        lax.all_to_all(jnp.stack([field] * lax.axis_size("ch")), "ch", 0, 0), axis=1
+    )
     return (smoothed_factor, new_channel)
 
 

time: 292 us -> 276 us (0.945)
  blocking collectives: 10.2 us -> 37.6 us
  waiting for transfers between devices: 154 us -> 127 us
  other arithmetic: 23.7 us -> 17.1 us
  local copies, waits for them, and re-layouts: 14.1 us -> 8.37 us
  starting transfers between devices: 41.8 us -> 36.6 us
    all_gather x1 -> x0, waiting for transfers between devices: 38.5 us -> none  [shards(): smoothed_factor = lax.all_gather(field, 'ch', axis=1, tiled=True)]
    all_to_all x0 -> x1, blocking collectives: none -> 27.3 us  [shards(): lax.all_to_all(jnp.stack([field] * lax.axis_size('ch')), 'ch', 0, 0)]
    div x3 -> x2, other arithmetic: 23.6 us -> 9.66 us  [smooth_once(): return combined / (1.0 + weights[0] + weights[1] + weights[2] + weights[3])]
    ppermute x8, waiting for transfers between devices: 5.83 us -> 19.3 us  [padded_2(): lax.ppermute(lax.slice_in_dim(block, 0, width, axis=dim), axis, backward)]
    another operation x0 -> x2, other arithmetic: none -> 7.25 us  [shards(): jnp.stack([field] * lax.axis_size('ch'))]
    ppermute x8, starting transfers between devices: 31 us -> 26 us  [padded_2(): lax.ppermute(lax.slice_in_dim(block, block.shape[dim] - width, None, axis...]
    unnamed x17 -> x9, local copies, waits for them, and re-layouts: 5.77 us -> 1.35 us
    div x1 -> x0, local copies, waits for them, and re-layouts: 3.47 us -> none  [smooth_once(): return combined / (1.0 + weights[0] + weights[1] + weights[2] + weights[3])]
  transfers between devices with their start and end apart: 19 -> 18, of which waited for: 11 -> 11; matrix products, arithmetic and copies ran while one was open for 1% -> 0% of each run, Pallas kernels for 0% -> 0%
where the time goes in v1:
time: 276 us; the launch traced here: 274 us
  waiting for transfers between devices  127 us (46%)
  blocking collectives  37.6 us (14%)
  starting transfers between devices  36.6 us (13%)
  matrix products  33 us (12%)
  other arithmetic  17.1 us (6%)
  between operations  14.4 us (5%)
  local copies, waits for them, and re-layouts  8.37 us (3%)
    psum x1, waiting for transfers between devices, shards(): chan_top, pixel_gram = lax.psum((chan_top, pixel_gram), ('row', 'col'))  91.5 us
    all_to_all x1, blocking collectives, shards(): lax.all_to_all(jnp.stack([field] * lax.axis_size('ch')), 'ch', 0, 0)  27.3 us
    ppermute x8, starting transfers between devices, padded_2(): lax.ppermute(lax.slice_in_dim(block, block.shape[dim] - width, None, axis...  26 us
    ppermute x8, waiting for transfers between devices, padded_2(): lax.ppermute(lax.slice_in_dim(block, 0, width, axis=dim), axis, backward)  19.3 us
    reduce_scatter x1, waiting for transfers between devices, shards(): lax.psum_scatter(part_top, 'ch', scatter_dimension=1, tiled=True)  13.5 us
    dot_general x1, matrix products, shards(): lax.dot_general(flat_pixel, flat_data, contraction, precision=precise, pr...  12.2 us
    dot_general x1, matrix products, shards(): jnp.dot(new_channel, flat_data, precision=precise, preferred_element_type...  11.4 us
    ppermute x8, starting transfers between devices, padded_2(): lax.ppermute(lax.slice_in_dim(block, 0, width, axis=dim), axis, backward)  10.3 us
  transfers between devices with their start and end apart: 18, of which 11 were waited for; matrix products, arithmetic and copies ran while one was open for 0% of the time, Pallas kernels for 0%

profile of v1, /device:TPU:0, one launch (start us, length us, event | category | flops | bytes accessed | tf_op | source)
XLA Modules:
  0.0 274.3 jit_solution(5186106116190904063)
XLA Ops:
  7.2 7.0 %fusion.43 = f32[64,64]{1,0:T(8,128)} fusion(f32[64,32,256]{2,1,0:T(8,128)} %param.5), kind=kOutput, calls=%fused_computation.66 | convolution fusion | flops 402653184 | bytes 2113536 | tf_op jit(solution)/shard_map/dot_general | solution.py:61
  14.2 12.2 %fusion.37 = f32[64,192]{1,0:T(8,128)} fusion(f32[192,32,256]{2,1,0:T(8,128)} %param.4, f32[64,32,256]{2,1,0:T(8,128)S(1)} %copy-done), kind=kOutput, calls=%fused_computation.63 | convolution fusion | flops 1207959552 | bytes 8437760 | tf_op jit(solution)/shard_map/dot_general | solution.py:58
  26.7 91.5 %all-reduce.3.cloned.1.call-done = (f32[64,64]{1,0:T(8,128)}, f32[64,192]{1,0:T(8,128)}) async-done(((f32[64,64]{1,0:T(8,128)}, f32[64,192]{1,0:T(8,128)}), (f32[64,64]{1,0:T(8,128)}, f32[64,192]{1,0:T(8,128)})) %all-reduce.3.cloned.1.call-update) | async-done | bytes 65552 | tf_op jit(solution)/shard_map/psum | solution.py:64
  119.3 11.4 %fusion = f32[64,32,256]{2,0,1:T(8,128)} fusion(f32[64,192]{1,0:T(8,128)S(1)} %fusion.42, f32[24,8,32,256]{3,2,1,0:T(8,128)} %bitcast.34), kind=kOutput, calls=%fused_computation | convolution fusion | flops 1207959552 | bytes 8437760 | tf_op jit(solution)/shard_map/dot_general | solution.py:75
  132.8 4.5 %collective-permute-start = (s32[1,256]{1,0:T(1,128)S(1)}, s32[1,256]{1,0:T(1,128)S(1)}, u32[]{:S(2)}, u32[]{:S(2)}) collective-permute-start(s32[1,256]{1,0:T(1,128)S(1)} %get-tuple-element.26), channel_id=1, source_target_pairs={{0,1},{1,8},{8,9},{9,16},{16,17},{17,24},{24,25},{2,3},{3,10},{10,... | collective-permute-start | bytes 3080 | tf_op jit(solution)/shard_map/ppermute | solution.py:15
  138.8 10.2 %psum.23 = f32[64,64]{1,0:T(8,128)S(1)} all-reduce(f32[64,64]{1,0:T(8,128)S(1)} %fusion.56), channel_id=1, replica_groups=mesh['row'=4,'col'=4,'ch'=2] {'ch'}, use_global_device_ids=true, to_apply=%region_3.0 | all-reduce | flops 4096 | bytes 32768 | tf_op jit(solution)/shard_map/psum | solution.py:85
  149.0 13.5 %reduce-scatter.2.cloned.1.call-done = f32[64,16,256]{2,0,1:T(8,128)} async-done(((f32[64,32,256]{2,0,1:T(8,128)}), f32[64,16,256]{2,0,1:T(8,128)}) %reduce-scatter.2.cloned.1.call-update) | async-done | bytes 1048592 | tf_op jit(solution)/shard_map/reduce_scatter | solution.py:84
  165.6 2.3 collective-permute-start.1
  170.6 3.0 %collective-permute-start.4 = (s32[18,1]{1,0:T(8,128)S(1)}, s32[18,1]{1,0:T(8,128)S(1)}, u32[]{:S(2)}, u32[]{:S(2)}) collective-permute-start(s32[18,1]{1,0:T(8,128)S(1)} %get-tuple-element.24), channel_id=1, source_target_pairs={{0,2},{2,4},{4,6},{1,3},{3,5},{5,7},{8,10},{10,12},{12,14},{9,11},... | collective-permute-start | bytes 224 | tf_op jit(solution)/shard_map/ppermute | solution.py:15
  178.3 3.3 %collective-permute-done.7 = f32[64,18,1]{0,2,1:T(1,128)S(1)} collective-permute-done((f32[64,18,1]{0,2,1:T(1,128)S(1)}, f32[64,18,1]{0,2,1:T(1,128)S(1)}, u32[]{:S(2)}, u32[]{:S(2)}) %collective-permute-start.7) | collective-permute-done | bytes 4640 | tf_op jit(solution)/shard_map/ppermute | solution.py:18
  181.6 4.8 %fusion.27 = f32[64,16,256]{0,2,1:T(8,128)S(1)} fusion(f32[64,18,1]{0,2,1:T(1,128)S(1)} %collective-permute-done.7, f32[64,1,256]{0,2,1:T(8,128)S(1)} %collective-permute-done.3, f32[64,16,256]{0,2,1:T(8,128)S(1)} %bitcast.37, f32[64,1,256]{0,2,1:T(8,128)S(1)} %collective-permute-done.1, f32[64,18,1]{0,2,1:T(1,128)S(1)} %collective-permute-done.5, ...), kind=kLoop, calls=%fused_computation.46 | loop fusion | flops 4456448 | bytes 2319360 | tf_op jit(solution)/shard_map/div | solution.py:38
  186.4 4.7 %collective-permute-start.8 = (f32[64,1,256]{0,2,1:T(8,128)S(1)}, f32[64,1,256]{0,2,1:T(8,128)S(1)}, u32[]{:S(2)}, u32[]{:S(2)}) collective-permute-start(f32[64,1,256]{0,2,1:T(8,128)S(1)} %get-tuple-element.19), channel_id=1, source_target_pairs={{0,1},{1,8},{8,9},{9,16},{16,17},{17,24},{24,25},{2,3},{3,10},{10,... | collective-permute-start | bytes 196616 | tf_op jit(solution)/shard_map/ppermute | solution.py:15
  193.6 4.6 %collective-permute-done.9 = f32[64,1,256]{0,2,1:T(8,128)S(1)} collective-permute-done((f32[64,1,256]{0,2,1:T(8,128)S(1)}, f32[64,1,256]{0,2,1:T(8,128)S(1)}, u32[]{:S(2)}, u32[]{:S(2)}) %collective-permute-start.9) | collective-permute-done | bytes 65568 | tf_op jit(solution)/shard_map/ppermute | solution.py:18
  198.3 2.9 %collective-permute-start.10 = (f32[64,18,1]{0,2,1:T(1,128)S(1)}, f32[64,18,1]{0,2,1:T(1,128)S(1)}, u32[]{:S(2)}, u32[]{:S(2)}) collective-permute-start(f32[64,18,1]{0,2,1:T(1,128)S(1)} %get-tuple-element.13), channel_id=1, source_target_pairs={{0,2},{2,4},{4,6},{1,3},{3,5},{5,7},{8,10},{10,12},{12,14},{9,11},... | collective-permute-start | bytes 13832 | tf_op jit(solution)/shard_map/ppermute | solution.py:15
  202.5 2.5 collective-permute-done.11
  204.9 4.8 %fusion.18 = f32[64,16,256]{0,2,1:T(8,128)S(1)} fusion(f32[64,18,1]{0,2,1:T(1,128)S(1)} %collective-permute-done.11, f32[64,1,256]{0,2,1:T(8,128)S(1)} %collective-permute-done.9, f32[64,16,256]{0,2,1:T(8,128)S(1)} %fusion.27, f32[64,1,256]{0,2,1:T(8,128)S(1)} %collective-permute-done.8, f32[64,18,1]{0,2,1:T(1,128)S(1)} %collective-permute-done.10, ...), kind=kLoop, calls=%fused_computation.29 | loop fusion | flops 4456448 | bytes 2319360 | tf_op jit(solution)/shard_map/div | solution.py:38
  209.8 4.3 %collective-permute-start.12 = (f32[64,1,256]{0,2,1:T(8,128)S(1)}, f32[64,1,256]{0,2,1:T(8,128)S(1)}, u32[]{:S(2)}, u32[]{:S(2)}) collective-permute-start(f32[64,1,256]{0,2,1:T(8,128)S(1)} %get-tuple-element.17), channel_id=1, source_target_pairs={{0,1},{1,8},{8,9},{9,16},{16,17},{17,24},{24,25},{2,3},{3,10},{10,... | collective-permute-start | bytes 196616 | tf_op jit(solution)/shard_map/ppermute | solution.py:15
  216.6 4.6 %collective-permute-done.13 = f32[64,1,256]{0,2,1:T(8,128)S(1)} collective-permute-done((f32[64,1,256]{0,2,1:T(8,128)S(1)}, f32[64,1,256]{0,2,1:T(8,128)S(1)}, u32[]{:S(2)}, u32[]{:S(2)}) %collective-permute-start.13) | collective-permute-done | bytes 65568 | tf_op jit(solution)/shard_map/ppermute | solution.py:18
  221.3 2.9 %collective-permute-start.14 = (f32[64,18,1]{0,2,1:T(1,128)S(1)}, f32[64,18,1]{0,2,1:T(1,128)S(1)}, u32[]{:S(2)}, u32[]{:S(2)}) collective-permute-start(f32[64,18,1]{0,2,1:T(1,128)S(1)} %get-tuple-element.11), channel_id=1, source_target_pairs={{0,2},{2,4},{4,6},{1,3},{3,5},{5,7},{8,10},{10,12},{12,14},{9,11},... | collective-permute-start | bytes 13832 | tf_op jit(solution)/shard_map/ppermute | solution.py:15
  225.5 2.5 collective-permute-done.15
  228.0 4.8 %fusion.9 = f32[1,64,16,256]{1,3,2,0:T(8,128)S(1)} fusion(f32[64,18,1]{0,2,1:T(1,128)S(1)} %collective-permute-done.15, f32[64,1,256]{0,2,1:T(8,128)S(1)} %collective-permute-done.13, f32[64,16,256]{0,2,1:T(8,128)S(1)} %fusion.18, f32[64,1,256]{0,2,1:T(8,128)S(1)} %collective-permute-done.12, f32[64,18,1]{0,2,1:T(1,128)S(1)} %collective-permute-done.14, ...), kind=kLoop, calls=%fused_computation.12 | loop fusion | flops 4456448 | bytes 2319360 | tf_op jit(solution)/shard_map/stack | solution.py:95
  232.8 2.4 pad_maximum_fusion
  235.2 3.4 %copy.52 = f32[2,64,16,256]{3,2,1,0:T(8,128)S(1)} copy(f32[2,64,16,256]{1,3,2,0:T(8,128)} %pad_maximum_fusion) | data formatting | bytes 4194304 | tf_op jit(solution)/shard_map/stack | solution.py:95
  238.6 27.3 %all_to_all.5 = f32[2,64,16,256]{3,2,1,0:T(8,128)S(1)} all-to-all(f32[2,64,16,256]{3,2,1,0:T(8,128)S(1)} %copy.52), channel_id=1, replica_groups=mesh['row'=4,'col'=4,'ch'=2] {'ch'}, dimensions={0} | all-to-all | bytes 4194304 | tf_op jit(solution)/shard_map/all_to_all | solution.py:95
  (51 shorter events, 24.3 us)
Async XLA Ops:
  7.2 7.1 %copy-start = (f32[64,32,256]{2,1,0:T(8,128)S(1)}, f32[64,32,256]{2,1,0:T(8,128)}, u32[]{:S(2)}) copy-start(f32[64,32,256]{2,1,0:T(8,128)} %param.5) | copy-start | bytes 6291460
  7.2 111.1 %all-reduce.3.cloned.1.call-start = ((), (), s32[]{:S(2)}) async-start(), calls=%async_computation.3 | async-start | bytes 196608 | tf_op jit(solution)/shard_map/psum | solution.py:64
  14.2 104.0 %copy-start.3 = (f32[64,192]{1,0:T(8,128)S(1)}, f32[64,192]{1,0:T(8,128)}, u32[]{:S(2)}) copy-start(f32[64,192]{1,0:T(8,128)} %param.6) | copy-start | bytes 147460
  26.5 136.1 %reduce-scatter.2.cloned.1.call-start = ((), (), s32[]{:S(2)}) async-start(), calls=%async_computation.2 | async-start | bytes 3145728 | tf_op jit(solution)/shard_map/reduce_scatter | solution.py:84
  119.3 19.3 %copy-start.1 = (f32[64,192]{1,0:T(8,128)}, f32[64,192]{1,0:T(8,128)S(1)}, u32[]{:S(2)}) copy-start(f32[64,192]{1,0:T(8,128)S(1)} %fusion.42) | copy-start | bytes 147460
  130.7 0.8 copy-start.2
  131.5 6.6 %collective-permute-start.2 = (s32[1,256]{1,0:T(1,128)S(1)}, s32[1,256]{1,0:T(1,128)S(1)}, u32[]{:S(2)}, u32[]{:S(2)}) collective-permute-start(s32[1,256]{1,0:T(1,128)S(1)} %get-tuple-element.25), channel_id=1, source_target_pairs={{1,0},{8,1},{9,8},{16,9},{17,16},{24,17},{25,24},{3,2},{10,3},{11,... | collective-permute-start | bytes 3080 | tf_op jit(solution)/shard_map/ppermute | solution.py:18
  132.8 5.8 %collective-permute-start = (s32[1,256]{1,0:T(1,128)S(1)}, s32[1,256]{1,0:T(1,128)S(1)}, u32[]{:S(2)}, u32[]{:S(2)}) collective-permute-start(s32[1,256]{1,0:T(1,128)S(1)} %get-tuple-element.26), channel_id=1, source_target_pairs={{0,1},{1,8},{8,9},{9,16},{16,17},{17,24},{24,25},{2,3},{3,10},{10,... | collective-permute-start | bytes 3080 | tf_op jit(solution)/shard_map/ppermute | solution.py:15
  165.6 8.0 %collective-permute-start.1 = (f32[64,1,256]{0,2,1:T(8,128)S(1)}, f32[64,1,256]{0,2,1:T(8,128)S(1)}, u32[]{:S(2)}, u32[]{:S(2)}) collective-permute-start(f32[64,1,256]{0,2,1:T(8,128)S(1)} %get-tuple-element.21), channel_id=1, source_target_pairs={{0,1},{1,8},{8,9},{9,16},{16,17},{17,24},{24,25},{2,3},{3,10},{10,... | collective-permute-start | bytes 196616 | tf_op jit(solution)/shard_map/ppermute | solution.py:15
  167.9 7.6 %collective-permute-start.3 = (f32[64,1,256]{0,2,1:T(8,128)S(1)}, f32[64,1,256]{0,2,1:T(8,128)S(1)}, u32[]{:S(2)}, u32[]{:S(2)}) collective-permute-start(f32[64,1,256]{0,2,1:T(8,128)S(1)} %get-tuple-element.22), channel_id=1, source_target_pairs={{1,0},{8,1},{9,8},{16,9},{17,16},{24,17},{25,24},{3,2},{10,3},{11,... | collective-permute-start | bytes 196616 | tf_op jit(solution)/shard_map/ppermute | solution.py:18
  169.3 8.9 %collective-permute-start.6 = (s32[18,1]{1,0:T(8,128)S(1)}, s32[18,1]{1,0:T(8,128)S(1)}, u32[]{:S(2)}, u32[]{:S(2)}) collective-permute-start(s32[18,1]{1,0:T(8,128)S(1)} %get-tuple-element.23), channel_id=1, source_target_pairs={{2,0},{4,2},{6,4},{3,1},{5,3},{7,5},{10,8},{12,10},{14,12},{11,9},... | collective-permute-start | bytes 224 | tf_op jit(solution)/shard_map/ppermute | solution.py:18
  170.6 7.6 %collective-permute-start.4 = (s32[18,1]{1,0:T(8,128)S(1)}, s32[18,1]{1,0:T(8,128)S(1)}, u32[]{:S(2)}, u32[]{:S(2)}) collective-permute-start(s32[18,1]{1,0:T(8,128)S(1)} %get-tuple-element.24), channel_id=1, source_target_pairs={{0,2},{2,4},{4,6},{1,3},{3,5},{5,7},{8,10},{10,12},{12,14},{9,11},... | collective-permute-start | bytes 224 | tf_op jit(solution)/shard_map/ppermute | solution.py:15
  175.5 2.8 %collective-permute-start.5 = (f32[64,18,1]{0,2,1:T(1,128)S(1)}, f32[64,18,1]{0,2,1:T(1,128)S(1)}, u32[]{:S(2)}, u32[]{:S(2)}) collective-permute-start(f32[64,18,1]{0,2,1:T(1,128)S(1)} %get-tuple-element.15), channel_id=1, source_target_pairs={{0,2},{2,4},{4,6},{1,3},{3,5},{5,7},{8,10},{10,12},{12,14},{9,11},... | collective-permute-start | bytes 13832 | tf_op jit(solution)/shard_map/ppermute | solution.py:15
  176.9 4.7 %collective-permute-start.7 = (f32[64,18,1]{0,2,1:T(1,128)S(1)}, f32[64,18,1]{0,2,1:T(1,128)S(1)}, u32[]{:S(2)}, u32[]{:S(2)}) collective-permute-start(f32[64,18,1]{0,2,1:T(1,128)S(1)} %get-tuple-element.16), channel_id=1, source_target_pairs={{2,0},{4,2},{6,4},{3,1},{5,3},{7,5},{10,8},{12,10},{14,12},{11,9},... | collective-permute-start | bytes 13832 | tf_op jit(solution)/shard_map/ppermute | solution.py:18
  186.4 7.2 %collective-permute-start.8 = (f32[64,1,256]{0,2,1:T(8,128)S(1)}, f32[64,1,256]{0,2,1:T(8,128)S(1)}, u32[]{:S(2)}, u32[]{:S(2)}) collective-permute-start(f32[64,1,256]{0,2,1:T(8,128)S(1)} %get-tuple-element.19), channel_id=1, source_target_pairs={{0,1},{1,8},{8,9},{9,16},{16,17},{17,24},{24,25},{2,3},{3,10},{10,... | collective-permute-start | bytes 196616 | tf_op jit(solution)/shard_map/ppermute | solution.py:15
  191.1 7.1 %collective-permute-start.9 = (f32[64,1,256]{0,2,1:T(8,128)S(1)}, f32[64,1,256]{0,2,1:T(8,128)S(1)}, u32[]{:S(2)}, u32[]{:S(2)}) collective-permute-start(f32[64,1,256]{0,2,1:T(8,128)S(1)} %get-tuple-element.20), channel_id=1, source_target_pairs={{1,0},{8,1},{9,8},{16,9},{17,16},{24,17},{25,24},{3,2},{10,3},{11,... | collective-permute-start | bytes 196616 | tf_op jit(solution)/shard_map/ppermute | solution.py:18
  198.3 4.2 %collective-permute-start.10 = (f32[64,18,1]{0,2,1:T(1,128)S(1)}, f32[64,18,1]{0,2,1:T(1,128)S(1)}, u32[]{:S(2)}, u32[]{:S(2)}) collective-permute-start(f32[64,18,1]{0,2,1:T(1,128)S(1)} %get-tuple-element.13), channel_id=1, source_target_pairs={{0,2},{2,4},{4,6},{1,3},{3,5},{5,7},{8,10},{10,12},{12,14},{9,11},... | collective-permute-start | bytes 13832 | tf_op jit(solution)/shard_map/ppermute | solution.py:15
  201.2 3.8 %collective-permute-start.11 = (f32[64,18,1]{0,2,1:T(1,128)S(1)}, f32[64,18,1]{0,2,1:T(1,128)S(1)}, u32[]{:S(2)}, u32[]{:S(2)}) collective-permute-start(f32[64,18,1]{0,2,1:T(1,128)S(1)} %get-tuple-element.14), channel_id=1, source_target_pairs={{2,0},{4,2},{6,4},{3,1},{5,3},{7,5},{10,8},{12,10},{14,12},{11,9},... | collective-permute-start | bytes 13832 | tf_op jit(solution)/shard_map/ppermute | solution.py:18
  209.8 6.8 %collective-permute-start.12 = (f32[64,1,256]{0,2,1:T(8,128)S(1)}, f32[64,1,256]{0,2,1:T(8,128)S(1)}, u32[]{:S(2)}, u32[]{:S(2)}) collective-permute-start(f32[64,1,256]{0,2,1:T(8,128)S(1)} %get-tuple-element.17), channel_id=1, source_target_pairs={{0,1},{1,8},{8,9},{9,16},{16,17},{17,24},{24,25},{2,3},{3,10},{10,... | collective-permute-start | bytes 196616 | tf_op jit(solution)/shard_map/ppermute | solution.py:15
  214.1 7.1 %collective-permute-start.13 = (f32[64,1,256]{0,2,1:T(8,128)S(1)}, f32[64,1,256]{0,2,1:T(8,128)S(1)}, u32[]{:S(2)}, u32[]{:S(2)}) collective-permute-start(f32[64,1,256]{0,2,1:T(8,128)S(1)} %get-tuple-element.18), channel_id=1, source_target_pairs={{1,0},{8,1},{9,8},{16,9},{17,16},{24,17},{25,24},{3,2},{10,3},{11,... | collective-permute-start | bytes 196616 | tf_op jit(solution)/shard_map/ppermute | solution.py:18
  221.3 4.2 %collective-permute-start.14 = (f32[64,18,1]{0,2,1:T(1,128)S(1)}, f32[64,18,1]{0,2,1:T(1,128)S(1)}, u32[]{:S(2)}, u32[]{:S(2)}) collective-permute-start(f32[64,18,1]{0,2,1:T(1,128)S(1)} %get-tuple-element.11), channel_id=1, source_target_pairs={{0,2},{2,4},{4,6},{1,3},{3,5},{5,7},{8,10},{10,12},{12,14},{9,11},... | collective-permute-start | bytes 13832 | tf_op jit(solution)/shard_map/ppermute | solution.py:15
  224.2 3.8 %collective-permute-start.15 = (f32[64,18,1]{0,2,1:T(1,128)S(1)}, f32[64,18,1]{0,2,1:T(1,128)S(1)}, u32[]{:S(2)}, u32[]{:S(2)}) collective-permute-start(f32[64,18,1]{0,2,1:T(1,128)S(1)} %get-tuple-element.12), channel_id=1, source_target_pairs={{2,0},{4,2},{6,4},{3,1},{5,3},{7,5},{10,8},{12,10},{14,12},{11,9},... | collective-permute-start | bytes 13832 | tf_op jit(solution)/shard_map/ppermute | solution.py:18
Sparse Core Ops, SparseCore 0:
  26.6 91.6 all-reduce.2
  130.8 31.6 reduce-scatter.1
